TPU v7x, 512 devices: a whole 4x4x16 slice. The times are simulated.
512 devices in a mesh: pack: 16 (over y, x), seq: 32 (over z, core).
Axes of the slice: x: 4, y: 4, z: 16, core: 2. Of those that a mesh axis runs over, the one named last changes fastest.
Arguments:
- queries: bfloat16 [65536, 2048], P(('pack', 'seq')), parts along dimension 0, may hold values from -48 to 48
- token_key_heads: bfloat16 [65536, 256], P(('pack', 'seq')), parts along dimension 0, may hold values from -6 to 6
- token_value_heads: bfloat16 [65536, 256], P(('pack', 'seq')), parts along dimension 0, may hold values from -6 to 6
- residual: bfloat16 [65536, 1024], P(('pack', 'seq')), parts along dimension 0, may hold values from -40 to 40
- out_weight: bfloat16 [2048, 1024], P('seq'), may hold values from -0.125 to 0.125
- norm_gain: bfloat16 [1024], replicated, may hold values from 0.5 to 1.5
- w_gate: bfloat16 [32, 1024, 384], P('seq'), may hold values from -0.1875 to 0.1875
- w_up: bfloat16 [32, 1024, 384], P('seq'), may hold values from -0.1875 to 0.1875
- w_down: bfloat16 [32, 384, 1024], P('seq'), may hold values from -0.3125 to 0.3125
- expert_ids: int32 [65536, 8], P(('pack', 'seq')), parts along dimension 0, may hold values from 0 to 31, all different within a row; in each aligned block of 128 rows (0 to 127, 128 to 255, ...) at most 48 rows name the same one
- gate_weights: float32 [65536, 8], P(('pack', 'seq')), parts along dimension 0, may hold values from 0.05 to 0.3
- doc_of_block: int32 [512], P('pack'), parts along dimension 0, may hold values from 0 to 7, never falling along the last dimension, each value on 1 to 8 neighbouring positions
Outputs:
- attention: bfloat16 [65536, 2048], P(('pack', 'seq')), parts along dimension 0
- hidden_out: bfloat16 [65536, 1024], P(('pack', 'seq')), parts along dimension 0
- expert_mix: bfloat16 [65536, 1024], P(('pack', 'seq')), parts along dimension 0
There are 16 independent parts, one for each index of `pack`. A program takes and returns all parts, laid end to end along the dimension named above; an argument that names none is the same for every part. Nothing has to cross between parts.
Inputs may be any that keep to these rules, and one draw needn't show every extreme that they name: `expert_ids`: each row names 8 different experts; within the rows of one block no expert is named more than 48 times, and in every draw some expert is named exactly 48 times by the rows of some block. `doc_of_block`: never falls from block to block; each document covers 1 to 8 blocks, one exactly 8.
All inputs are finite; a program needn't handle non-finite values.
Results may differ from a plain program's by a relative error of at most 0.015.
Values may be sent and summed in bfloat16 or wider, within the bound.
A program may use at most 64 MiB of HBM per device.

v0:
```python
import math
import jax
import jax.numpy as jnp
from jax import lax
from jax.sharding import PartitionSpec as P

QUERY_HEADS = 16
KEY_VALUE_HEADS = 2
HEAD_SIZE = 128
TOP = 8


def attend(queries, key_token_rows, value_token_rows, query_pos, key_pos, allowed):
    token_rows = queries.shape[0]
    heads_per_group = QUERY_HEADS // KEY_VALUE_HEADS
    token_query_heads = queries.reshape(token_rows, KEY_VALUE_HEADS, heads_per_group, HEAD_SIZE)
    key_count = key_token_rows.shape[0]
    tile_length = math.gcd(key_count, 512)
    number_of_tiles = key_count // tile_length
    key_tile_list = key_token_rows.reshape(number_of_tiles, tile_length, KEY_VALUE_HEADS, HEAD_SIZE)
    value_tile_list = value_token_rows.reshape(
        number_of_tiles, tile_length, KEY_VALUE_HEADS, HEAD_SIZE
    )
    pos_tiles = key_pos.reshape(number_of_tiles, tile_length)
    allowed_tiles = allowed.reshape(number_of_tiles, tile_length)
    factor = 1.0 / HEAD_SIZE**0.5

    def tile_step(running, tile):
        key_tile, value_tile, pos_tile, allowed_tile = tile
        visible = allowed_tile[None, :] & (pos_tile[None, :] <= query_pos[:, None])

        def compute(current):
            run_max, run_sum, accum = current
            scores = (
                jnp.einsum(
                    "tkgd,skd->kgts",
                    token_query_heads,
                    key_tile,
                    preferred_element_type=jnp.float32,
                )
                * factor
            )
            scores = jnp.where(visible, scores, -1e30)
            new_max = jnp.maximum(run_max, jnp.max(scores, axis=-1))
            terms = jnp.where(visible, jnp.exp(scores - new_max[..., None]), 0.0)
            rescale = jnp.exp(run_max - new_max)
            new_sum = run_sum * rescale + jnp.sum(terms, axis=-1)
            product = jnp.einsum(
                "kgts,skd->kgtd",
                terms.astype(jnp.bfloat16),
                value_tile,
                preferred_element_type=jnp.float32,
            )
            return (new_max, new_sum, accum * rescale[..., None] + product)

        return (lax.cond(jnp.any(visible), compute, lambda current: current, running), None)

    start_state = (
        jnp.full((KEY_VALUE_HEADS, heads_per_group, token_rows), -1e30, jnp.float32),
        jnp.zeros((KEY_VALUE_HEADS, heads_per_group, token_rows), jnp.float32),
        jnp.zeros((KEY_VALUE_HEADS, heads_per_group, token_rows, HEAD_SIZE), jnp.float32),
    )
    final_state, _ = lax.scan(
        tile_step, start_state, (key_tile_list, value_tile_list, pos_tiles, allowed_tiles)
    )
    run_max, run_sum, accum = final_state
    result = accum / run_sum[..., None]
    return (
        jnp.transpose(result, (2, 0, 1, 3))
        .reshape(token_rows, QUERY_HEADS * HEAD_SIZE)
        .astype(jnp.bfloat16)
    )


def expert_rows(arrived, gate_proj, up_proj, down_proj):
    sources, slot_count, width = arrived.shape
    flat_rows = arrived.reshape(sources * slot_count, width)
    gate_part = jnp.dot(flat_rows, gate_proj, preferred_element_type=jnp.float32)
    up_part = jnp.dot(flat_rows, up_proj, preferred_element_type=jnp.float32)
    activated = (jax.nn.silu(gate_part) * up_part).astype(jnp.bfloat16)
    produced = jnp.dot(activated, down_proj, preferred_element_type=jnp.float32).astype(
        jnp.bfloat16
    )
    return produced.reshape(sources, slot_count, width)


def shards(
    queries,
    token_key_heads,
    token_value_heads,
    residual,
    out_weight,
    norm_gain,
    w_gate,
    w_up,
    w_down,
    expert_ids,
    gate_weights,
    doc_of_block,
):
    token_rows = queries.shape[0]
    blocks = lax.axis_size("seq")
    own_index = lax.axis_index("seq")
    local_pos = jnp.arange(token_rows, dtype=jnp.int32)
    query_pos = own_index * token_rows + local_pos
    own_doc = doc_of_block[own_index]
    key_head_width = token_key_heads.shape[1]
    key_token_rows, value_token_rows = (
        lax.all_gather(token_key_heads, "seq", axis=0, tiled=True),
        lax.all_gather(token_value_heads, "seq", axis=0, tiled=True),
    )
    key_pos = jnp.arange(blocks * token_rows, dtype=jnp.int32)
    key_block = key_pos // token_rows
    allowed = (key_block <= own_index) & ((doc_of_block[key_block] == own_doc) | (key_block == 0))
    key_token_rows = key_token_rows.reshape(
        key_token_rows.shape[0], KEY_VALUE_HEADS, key_head_width // KEY_VALUE_HEADS
    )
    value_token_rows = value_token_rows.reshape(
        value_token_rows.shape[0], KEY_VALUE_HEADS, key_head_width // KEY_VALUE_HEADS
    )
    attention = attend(queries, key_token_rows, value_token_rows, query_pos, key_pos, allowed)
    width = residual.shape[1]
    projected = jnp.dot(
        attention,
        lax.all_gather(out_weight, "seq", axis=0, tiled=True),
        preferred_element_type=jnp.float32,
    )
    hidden_state = residual.astype(jnp.float32) + projected
    mean_square = jnp.mean(hidden_state * hidden_state, axis=-1, keepdims=True)
    normed = (hidden_state * lax.rsqrt(mean_square + 1e-06) * norm_gain.astype(jnp.float32)).astype(
        jnp.bfloat16
    )
    slot_cap = min(token_rows, 3 * token_rows * TOP // (2 * blocks))
    routed_ids = expert_ids.reshape(-1)
    one_hot = (routed_ids[:, None] == jnp.arange(blocks, dtype=jnp.int32)[None, :]).astype(
        jnp.int32
    )
    earlier = jnp.cumsum(one_hot, axis=0) - one_hot
    slot_pos = jnp.sum(earlier * one_hot, axis=1)
    slot_index = routed_ids * slot_cap + slot_pos
    token_of = jnp.arange(token_rows * TOP, dtype=jnp.int32) // TOP
    outgoing = (
        jnp.zeros((blocks * slot_cap, width), jnp.bfloat16).at[slot_index].set(normed[token_of])
    )
    outgoing = outgoing.reshape(blocks, slot_cap, width)
    arrived = lax.all_to_all(outgoing, "seq", split_axis=0, concat_axis=0, tiled=True)
    served = expert_rows(arrived, w_gate[0], w_up[0], w_down[0])
    returned_rows = lax.all_to_all(served, "seq", split_axis=0, concat_axis=0, tiled=True)
    picked = returned_rows.reshape(blocks * slot_cap, width)[slot_index].astype(jnp.float32)
    weighted = picked * gate_weights.reshape(-1)[:, None]
    expert_mix = jnp.sum(weighted.reshape(token_rows, TOP, width), axis=1).astype(jnp.bfloat16)
    return (attention, hidden_state.astype(jnp.bfloat16), expert_mix)


def solution(mesh):
    in_specs = (
        P(("pack", "seq"), None),
        P(("pack", "seq"), None),
        P(("pack", "seq"), None),
        P(("pack", "seq"), None),
        P("seq", None),
        P(),
        P("seq", None, None),
        P("seq", None, None),
        P("seq", None, None),
        P(("pack", "seq"), None),
        P(("pack", "seq"), None),
        P("pack"),
    )
    out_specs = (P(("pack", "seq"), None), P(("pack", "seq"), None), P(("pack", "seq"), None))
    return jax.shard_map(shards, mesh=mesh, in_specs=in_specs, out_specs=out_specs, check_vma=False)
```

profile of v0, /device:TPU:4, one launch (start us, length us, event | category | flops | bytes accessed | tf_op | source)
XLA Modules:
  0.0 583.3 jit_solution(16247242193508925619)
XLA Ops:
  7.2 0.7 all-gather.4.cloned.1.call-update
  8.0 0.7 all-gather.6.cloned.1.call-update
  8.7 0.7 all-gather.8.cloned.1.call-update
  9.4 0.8 copy.27
  11.9 1.9 fusion.43
  13.8 2.1 fusion.42
  15.8 4.5 compare_select_fusion.1
  20.3 16.1 %select_compare_fusion = pred[4096]{0:T(1024)(128)(4,1)S(1)} fusion(pred[4096]{0:T(1024)(128)(4,1)S(1)} %compare_reduce_fusion, pred[4096]{0:T(1024)(128)(4,1)S(1)} %compare_reduce_fusion.1, pred[4096]{0:T(1024)(128)(4,1)S(1)} %compare_reduce_fusion.2, pred[4096]{0:T(1024)(128)(4,1)S(1)} %compare_reduce_fusion.3, ...), kind=kLoop, calls=%fused_computation.99 | loop fusion | flops 106496 | bytes 122984 | tf_op jit(solution)/shard_map/eq | solution.py:114
  36.4 1.3 copy.20
  37.8 0.3 copy.23
  38.1 0.7 convert_element_type.59
  38.8 9.0 %reduce-window.6 = s32[32,8,128]{2,1,0:T(8,128)S(1)} reduce-window(s32[32,8,128]{2,1,0:T(8,128)S(1)} %fusion.37, s32[]{:T(128)} %copy.62), window={size=1x1x128 pad=0_0x0_0x127_0}, to_apply=%region_7.8 | reduce-window | flops 4161536 | bytes 262148 | tf_op jit(solution)/shard_map/reduce-window
  47.9 0.1 copy.29
  48.1 0.1 copy.26
  48.6 37.9 %all-gather.4.cloned.1.call-done = bf16[4096,256]{1,0:T(8,128)(2,1)} async-done(((bf16[128,256]{1,0:T(8,128)(2,1)}), bf16[4096,256]{1,0:T(8,128)(2,1)}) %all-gather.4.cloned.1.call-update) | async-done | bytes 2097168 | tf_op jit(solution)/shard_map/all_gather | solution.py:109
  86.5 2.5 reshape.356
  89.0 1.8 copy.22
  90.8 66.5 %all-gather.6.cloned.1.call-done = bf16[4096,256]{1,0:T(8,128)(2,1)} async-done(((bf16[128,256]{1,0:T(8,128)(2,1)}), bf16[4096,256]{1,0:T(8,128)(2,1)}) %all-gather.6.cloned.1.call-update) | async-done | bytes 2097168 | tf_op jit(solution)/shard_map/all_gather | solution.py:110
  157.3 2.5 reshape.357
  159.9 1.8 copy.24
  161.7 18.0 %while.15 = (s32[]{:T(128)}, f32[2,8,128]{2,1,0:T(8,128)S(1)}, f32[2,8,128]{2,1,0:T(8,128)S(1)}, f32[2,8,128,128]{3,2,1,0:T(8,128)S(1)}, pred[8,512]{1,0:T(8,128...) while((s32[]{:T(128)}, f32[2,8,128]{2,1,0:T(8,128)S(1)}, ...), condition=%wide.region_6.7_spmd.clone, body=%wide.region_0.6_spmd.clone.sunk | while | flops 551227520 | bytes 16131831 | solution.py:63
  161.8 0.8 compare_and_fusion.2
  163.3 5.4 conditional.3
  163.3 1.7 fusion.2
  165.0 1.0 fusion.4
  166.0 2.6 fusion.8
  168.8 0.8 compare_and_fusion.2
  170.4 0.8 compare_and_fusion.2
  171.9 0.8 compare_and_fusion.2
  173.5 0.8 compare_and_fusion.2
  175.1 0.8 compare_and_fusion.2
  176.7 0.8 compare_and_fusion.2
  178.3 0.8 compare_and_fusion.2
  179.8 0.3 fusion.33
  180.1 0.3 copy.25
  180.5 0.1 copy.43
  180.7 49.5 %all-gather.8.cloned.1.call-done = bf16[2048,1024]{1,0:T(8,128)(2,1)} async-done(((bf16[64,1024]{1,0:T(8,128)(2,1)}), bf16[2048,1024]{1,0:T(8,128)(2,1)}) %all-gather.8.cloned.1.call-update) | async-done | bytes 4194320 | tf_op jit(solution)/shard_map/all_gather | solution.py:125
  230.1 3.0 multiply_reduce_fusion
  233.2 0.8 multiply_convert_fusion
  233.9 14.9 %scatter_custom_fusion = bf16[1536,1024]{1,0:T(8,128)(2,1)} fusion(s32[1024]{0:T(1024)S(1)} %bitcast.128, bf16[128,1024]{1,0:T(8,128)(2,1)S(1)} %get-tuple-element.196, s32[1024]{0:T(1024)S(1)} %broadcast_clamp_fusion.1, bf16[]{:T(256)} %constant.107.clone.1), kind=kCustom, calls=%fused_computation.34 | custom fusion | bytes 3145730 | tf_op jit(solution)/shard_map/scatter | solution.py:143
  248.9 154.5 %all_to_all.10 = bf16[32,48,1024]{2,1,0:T(8,128)(2,1)S(1)} all-to-all(bf16[32,48,1024]{2,1,0:T(8,128)(2,1)} %bitcast.115), channel_id=1, replica_groups=mesh['pack'=16,'seq'=32] {'seq'}, dimensions={0} | all-to-all | bytes 6291456 | tf_op jit(solution)/shard_map/all_to_all | solution.py:146
  403.4 1.7 copy-done.1
  405.1 3.2 fusion.31
  408.3 7.8 %convolution_convert_fusion = bf16[1536,1024]{1,0:T(8,128)(2,1)} fusion(bf16[1536,1024]{1,0:T(8,128)(2,1)} %bitcast.118, f32[1536,384]{1,0:T(8,128)} %fusion.31, bf16[1,384,1024]{2,1,0:T(8,128)(2,1)S(1)} %copy-done, bf16[1,1024,384]{2,1,0:T(8,128)(2,1)S(1)} %copy-done.7), kind=kOutput, calls=%fused_computation.31 | convolution fusion | flops 2421030912 | bytes 10223616 | tf_op jit(solution)/shard_map/dot_general | solution.py:81
  416.1 4.9 all-to-all-start.1
  421.2 146.3 %all-to-all-done.1 = bf16[32,48,1024]{2,1,0:T(8,128)(2,1)} async-done(((bf16[32,48,1024]{2,1,0:T(8,128)(2,1)}), bf16[32,48,1024]{2,1,0:T(8,128)(2,1)}, u32[]{:S(2)}, u32[]{:S(2)}) %all-to-all-start.1) | async-done | bytes 3145760 | tf_op jit(solution)/shard_map/all_to_all | solution.py:148
  567.5 7.3 %gather_fusion = bf16[1024,1024]{1,0:T(8,128)(2,1)S(1)} fusion(bf16[1536,1024]{1,0:T(8,128)(2,1)} %bitcast.54, s32[1024]{0:T(1024)S(1)} %broadcast_clamp_fusion), kind=kCustom, calls=%fused_computation.1 | custom fusion | bytes 4198400 | tf_op jit(solution)/shard_map/gather | solution.py:149
  574.8 2.0 fusion.22
  (100 shorter events, 2.9 us)
Async XLA Ops:
  7.2 401.2 %copy-start = (bf16[1,384,1024]{2,1,0:T(8,128)(2,1)S(1)}, bf16[1,384,1024]{2,1,0:T(8,128)(2,1)}, u32[]{:S(2)}) copy-start(bf16[1,384,1024]{2,1,0:T(8,128)(2,1)} %param.24) | copy-start | bytes 2359300
  7.2 40.9 %copy-start.4 = (s32[128,8]{0,1:T(8,128)S(1)}, s32[128,8]{0,1:T(8,128)}, u32[]{:S(2)}) copy-start(s32[128,8]{0,1:T(8,128)} %param.25) | copy-start | bytes 12292
  7.2 79.3 %all-gather.4.cloned.1.call-start = ((), (), s32[]{:S(2)}) async-start(), calls=%async_computation.2 | async-start | bytes 2162688 | tf_op jit(solution)/shard_map/all_gather | solution.py:109
  7.9 149.4 %all-gather.6.cloned.1.call-start = ((), (), s32[]{:S(2)}) async-start(), calls=%async_computation.3 | async-start | bytes 2162688 | tf_op jit(solution)/shard_map/all_gather | solution.py:110
  8.7 221.5 %all-gather.8.cloned.1.call-start = ((), (), s32[]{:S(2)}) async-start(), calls=%async_computation.4 | async-start | bytes 4325376 | tf_op jit(solution)/shard_map/all_gather | solution.py:125
  179.8 50.4 %copy-start.3 = (bf16[128,1024]{1,0:T(8,128)(2,1)S(1)}, bf16[128,1024]{1,0:T(8,128)(2,1)}, u32[]{:S(2)}) copy-start(bf16[128,1024]{1,0:T(8,128)(2,1)} %param.19) | copy-start | bytes 786436
  180.6 53.3 %copy-start.2 = (bf16[16,8,16,128]{3,1,2,0:T(8,128)(2,1)}, bf16[16,8,16,128]{3,1,2,0:T(8,128)(2,1)S(1)}, u32[]{:S(2)}) copy-start(bf16[16,8,16,128]{3,1,2,0:T(8,128)(2,1)S(1)} %copy.43) | copy-start | bytes 1572868
  248.9 156.2 %copy-start.6 = (bf16[1,1024,384]{2,1,0:T(8,128)(2,1)S(1)}, bf16[1,1024,384]{2,1,0:T(8,128)(2,1)}, u32[]{:S(2)}) copy-start(bf16[1,1024,384]{2,1,0:T(8,128)(2,1)} %param.22) | copy-start | bytes 2359300
  403.4 1.7 copy-start.1
  405.1 3.3 copy-start.7
  416.1 5.0 copy-start.5
  416.1 151.3 %all-to-all-start.1 = ((bf16[32,48,1024]{2,1,0:T(8,128)(2,1)}), bf16[32,48,1024]{2,1,0:T(8,128)(2,1)}, u32[]{:S(2)}, u32[]{:S(2)}) async-start(bf16[32,48,1024]{2,1,0:T(8,128)(2,1)} %bitcast.116), calls=%async_computation.1 | async-start | bytes 6291456 | tf_op jit(solution)/shard_map/all_to_all | solution.py:148
Sparse Core Ops, SparseCore 0:
  10.1 76.2 all-gather.3
  88.6 68.6 all-gather.5
  159.4 70.6 all-gather.7
where the time goes:
time: 584 us; the launch traced here: 583 us
  waiting for transfers between devices  302 us (52%)
  blocking collectives  155 us (27%)
  other arithmetic  42.8 us (7%)
  local copies, waits for them, and re-layouts  40.6 us (7%)
  matrix products  18.4 us (3%)
  between operations  14 us (2%)
    all_to_all x1, blocking collectives, shards(): lax.all_to_all(outgoing, 'seq', split_axis=0, concat_axis=0, tiled=True)  155 us
    all_to_all x1, waiting for transfers between devices, shards(): lax.all_to_all(served, 'seq', split_axis=0, concat_axis=0, tiled=True)  146 us
    all_gather x1, waiting for transfers between devices, shards(): lax.all_gather(token_value_heads, 'seq', axis=0, tiled=True)  66.5 us
    all_gather x1, waiting for transfers between devices, shards(): lax.all_gather(out_weight, 'seq', axis=0, tiled=True)  49.5 us
    all_gather x1, waiting for transfers between devices, shards(): lax.all_gather(token_key_heads, 'seq', axis=0, tiled=True)  37.9 us
    eq x1, other arithmetic, shards(): doc_of_block[key_block] == own_doc  16.1 us
    scatter x1, local copies, waits for them, and re-layouts, shards(): jnp.zeros((blocks * slot_cap, width), jnp.bfloat16).at[slot_index]  14.9 us
  transfers between devices with their start and end apart: 4, of which 4 were waited for; matrix products, arithmetic and copies ran while one was open for 10% of the time, Pallas kernels for 0%

commit v1 on v0

--- a/solution.py
+++ b/solution.py
@@ -1,13 +1,23 @@
+import functools
 import math
 import jax
 import jax.numpy as jnp
 from jax import lax
 from jax.sharding import PartitionSpec as P
+from jax.lax import all_to_all, axis_size
 
 QUERY_HEADS = 16
 KEY_VALUE_HEADS = 2
 HEAD_SIZE = 128
 TOP = 8
+
+
+def panel_connect(payload, link_axis):
+    r1 = jnp.concatenate(axis_size(link_axis) * [payload], axis=0)
+    return all_to_all(r1, axis_name=link_axis, split_axis=0, concat_axis=0, tiled=True)
+
+
+marks_plan = functools.partial(panel_connect, link_axis="seq")
 
 
 def attend(queries, key_token_rows, value_token_rows, query_pos, key_pos, allowed):
@@ -107,7 +117,7 @@
     key_head_width = token_key_heads.shape[1]
     key_token_rows, value_token_rows = (
         lax.all_gather(token_key_heads, "seq", axis=0, tiled=True),
-        lax.all_gather(token_value_heads, "seq", axis=0, tiled=True),
+        marks_plan(token_value_heads),
     )
     key_pos = jnp.arange(blocks * token_rows, dtype=jnp.int32)
     key_block = key_pos // token_rows

time: 584 us -> 554 us (0.949)
  the two profiles are of different devices: /device:TPU:4 before, /device:TPU:12 now
where the time goes in v1:
time: 554 us; the launch traced here: 551 us
  waiting for transfers between devices  209 us (38%)
  blocking collectives  154 us (28%)
  local copies, waits for them, and re-layouts  74.6 us (13%)
  other arithmetic  54.2 us (10%)
  starting transfers between devices  20.6 us (4%)
  matrix products  18.4 us (3%)
  between operations  14.4 us (3%)
  loops' own time  5.58 us (1%)
    all_to_all x1, blocking collectives, shards(): lax.all_to_all(outgoing, 'seq', split_axis=0, concat_axis=0, tiled=True)  154 us
    all_to_all x1, waiting for transfers between devices, shards(): lax.all_to_all(served, 'seq', split_axis=0, concat_axis=0, tiled=True)  146 us
    all_to_all x1, waiting for transfers between devices, panel_connect(): all_to_all(r1, axis_name=link_axis, split_axis=0, concat_axis=0, tiled=True)  24.4 us
    unnamed x64, local copies, waits for them, and re-layouts  24.3 us
    all_gather x1, waiting for transfers between devices, shards(): lax.all_gather(token_key_heads, 'seq', axis=0, tiled=True)  21.7 us
    eq x1, other arithmetic, shards(): doc_of_block[key_block] == own_doc  16.2 us
    another operation x3, other arithmetic  15.8 us
    all_to_all x1, starting transfers between devices, panel_connect(): all_to_all(r1, axis_name=link_axis, split_axis=0, concat_axis=0, tiled=True)  15.6 us
  transfers between devices with their start and end apart: 4, of which 4 were waited for; matrix products, arithmetic and copies ran while one was open for 19% of the time, Pallas kernels for 0%

profile of v1, /device:TPU:12, one launch (start us, length us, event | category | flops | bytes accessed | tf_op | source)
XLA Modules:
  0.0 550.6 jit_solution(1828405874058859242)
XLA Ops:
  7.9 0.8 constant_dynamic-update-slice_fusion.31
  8.8 0.8 constant_dynamic-update-slice_fusion.30
  9.6 0.8 constant_dynamic-update-slice_fusion.29
  10.5 0.8 constant_dynamic-update-slice_fusion.28
  11.3 0.8 constant_dynamic-update-slice_fusion.27
  12.1 0.8 constant_dynamic-update-slice_fusion.26
  13.0 0.8 constant_dynamic-update-slice_fusion.25
  13.8 0.8 constant_dynamic-update-slice_fusion.24
  14.7 0.8 constant_dynamic-update-slice_fusion.23
  15.5 0.8 constant_dynamic-update-slice_fusion.22
  16.4 0.8 constant_dynamic-update-slice_fusion.21
  17.2 0.8 constant_dynamic-update-slice_fusion.20
  18.1 0.8 constant_dynamic-update-slice_fusion.19
  19.7 0.8 constant_dynamic-update-slice_fusion.17
  21.7 2.9 copy.49
  24.6 15.6 %all-to-all-start = ((bf16[32,128,256]{1,2,0:T(8,128)(2,1)}), bf16[32,128,256]{1,2,0:T(8,128)(2,1)S(1)}, u32[]{:S(2)}, u32[]{:S(2)}) async-start(bf16[32,128,256]{1,2,0:T(8,128)(2,1)} %copy.49), calls=%async_computation | async-start | bytes 4194304 | tf_op jit(solution)/shard_map/all_to_all | solution.py:17
  44.9 4.5 compare_select_fusion.1
  49.4 16.2 %select_compare_fusion = pred[4096]{0:T(1024)(128)(4,1)S(1)} fusion(pred[4096]{0:T(1024)(128)(4,1)S(1)} %compare_reduce_fusion, pred[4096]{0:T(1024)(128)(4,1)S(1)} %compare_reduce_fusion.1, pred[4096]{0:T(1024)(128)(4,1)S(1)} %compare_reduce_fusion.2, pred[4096]{0:T(1024)(128)(4,1)S(1)} %compare_reduce_fusion.3, ...), kind=kLoop, calls=%fused_computation.131 | loop fusion | flops 106496 | bytes 122984 | tf_op jit(solution)/shard_map/eq | solution.py:124
  66.2 1.0 copy.48
  67.2 1.3 copy.52
  69.8 15.7 %reduce-window.6 = s32[32,8,128]{2,1,0:T(8,128)S(1)} reduce-window(s32[32,8,128]{2,1,0:T(8,128)} %fusion.37, s32[]{:T(128)} %copy.120), window={size=1x1x128 pad=0_0x0_0x127_0}, to_apply=%region_7.8 | reduce-window | flops 4161536 | bytes 262148 | tf_op jit(solution)/shard_map/reduce-window
  86.2 1.0 copy.58
  88.6 1.3 broadcast_multiply_fusion
  89.9 1.4 copy.55
  91.3 1.5 mul.85
  95.7 21.7 %all-gather.3.cloned.1.call-done = bf16[4096,256]{1,0:T(8,128)(2,1)} async-done(((bf16[128,256]{1,0:T(8,128)(2,1)}), bf16[4096,256]{1,0:T(8,128)(2,1)}) %all-gather.3.cloned.1.call-update) | async-done | bytes 2097168 | tf_op jit(solution)/shard_map/all_gather | solution.py:119
  117.4 4.0 reshape.359
  121.4 3.4 copy.51
  124.8 24.4 %all-to-all-done = bf16[32,128,256]{1,2,0:T(8,128)(2,1)S(1)} async-done(((bf16[32,128,256]{1,2,0:T(8,128)(2,1)}), bf16[32,128,256]{1,2,0:T(8,128)(2,1)S(1)}, u32[]{:S(2)}, u32[]{:S(2)}) %all-to-all-start) | async-done | bytes 2097184 | tf_op jit(solution)/shard_map/all_to_all | solution.py:17
  149.2 2.7 copy.50
  151.9 3.1 reshape_reshape.7
  155.0 3.0 copy.53
  158.1 23.7 %while.15 = (s32[]{:T(128)}, f32[2,8,128]{2,1,0:T(8,128)S(1)}, f32[2,8,128]{2,1,0:T(8,128)S(1)}, f32[2,8,128,128]{3,2,1,0:T(8,128)S(1)}, pred[8,512]{1,0:T(8,128...) while((s32[]{:T(128)}, f32[2,8,128]{2,1,0:T(8,128)S(1)}, ...), condition=%wide.region_6.7_spmd.clone, body=%wide.region_0.6_spmd.clone.sunk | while | flops 551227520 | bytes 16131831 | solution.py:73
  160.4 5.4 conditional.3
  160.4 1.7 fusion.2
  162.1 1.0 fusion.4
  163.1 2.6 fusion.8
  182.7 15.1 %all-gather.5.cloned.1.call-done = bf16[2048,1024]{1,0:T(8,128)(2,1)} async-done(((bf16[64,1024]{1,0:T(8,128)(2,1)}), bf16[2048,1024]{1,0:T(8,128)(2,1)}) %all-gather.5.cloned.1.call-update) | async-done | bytes 4194320 | tf_op jit(solution)/shard_map/all_gather | solution.py:135
  197.7 3.0 multiply_reduce_fusion
  201.5 15.0 %scatter_custom_fusion = bf16[1536,1024]{1,0:T(8,128)(2,1)} fusion(s32[1024]{0:T(1024)S(1)} %bitcast.132, bf16[128,1024]{1,0:T(8,128)(2,1)S(1)} %get-tuple-element.216, s32[1024]{0:T(1024)S(1)} %broadcast_clamp_fusion.1, bf16[]{:T(256)} %constant.107.clone.1), kind=kCustom, calls=%fused_computation.34 | custom fusion | bytes 3145730 | tf_op jit(solution)/shard_map/scatter | solution.py:153
  216.5 153.9 %all_to_all.19 = bf16[32,48,1024]{2,1,0:T(8,128)(2,1)S(1)} all-to-all(bf16[32,48,1024]{2,1,0:T(8,128)(2,1)} %bitcast.118), channel_id=1, replica_groups=mesh['pack'=16,'seq'=32] {'seq'}, dimensions={0} | all-to-all | bytes 6291456 | tf_op jit(solution)/shard_map/all_to_all | solution.py:156
  370.4 1.7 copy-done.2
  372.1 3.3 fusion.31
  375.4 7.8 %convolution_convert_fusion = bf16[1536,1024]{1,0:T(8,128)(2,1)} fusion(bf16[1536,1024]{1,0:T(8,128)(2,1)} %bitcast.121, f32[1536,384]{1,0:T(8,128)} %fusion.31, bf16[1,384,1024]{2,1,0:T(8,128)(2,1)S(1)} %copy-done, bf16[1,1024,384]{2,1,0:T(8,128)(2,1)S(1)} %copy-done.12), kind=kOutput, calls=%fused_computation.31 | convolution fusion | flops 2421030912 | bytes 10223616 | tf_op jit(solution)/shard_map/dot_general | solution.py:91
  383.1 4.9 all-to-all-start.2
  388.2 146.3 %all-to-all-done.2 = bf16[32,48,1024]{2,1,0:T(8,128)(2,1)} async-done(((bf16[32,48,1024]{2,1,0:T(8,128)(2,1)}), bf16[32,48,1024]{2,1,0:T(8,128)(2,1)}, u32[]{:S(2)}, u32[]{:S(2)}) %all-to-all-start.2) | async-done | bytes 3145760 | tf_op jit(solution)/shard_map/all_to_all | solution.py:158
  534.5 7.3 %gather_fusion = bf16[1024,1024]{1,0:T(8,128)(2,1)S(1)} fusion(bf16[1536,1024]{1,0:T(8,128)(2,1)} %bitcast.55, s32[1024]{0:T(1024)S(1)} %broadcast_clamp_fusion), kind=kCustom, calls=%fused_computation.1 | custom fusion | bytes 4198400 | tf_op jit(solution)/shard_map/gather | solution.py:159
  541.8 2.0 fusion.22
  (143 shorter events, 28.7 us)
Async XLA Ops:
  7.2 368.2 %copy-start = (bf16[1,384,1024]{2,1,0:T(8,128)(2,1)S(1)}, bf16[1,384,1024]{2,1,0:T(8,128)(2,1)}, u32[]{:S(2)}) copy-start(bf16[1,384,1024]{2,1,0:T(8,128)(2,1)} %param.24) | copy-start | bytes 2359300
  7.2 14.3 %copy-start.1 = (bf16[128,256]{1,0:T(8,128)(2,1)S(1)}, bf16[128,256]{1,0:T(8,128)(2,1)}, u32[]{:S(2)}) copy-start(bf16[128,256]{1,0:T(8,128)(2,1)} %param.18) | copy-start | bytes 196612
  7.2 110.2 %all-gather.3.cloned.1.call-start = ((), (), s32[]{:S(2)}) async-start(), calls=%async_computation.3 | async-start | bytes 2162688 | tf_op jit(solution)/shard_map/all_gather | solution.py:119
  24.6 16.4 %copy-start.8 = (s32[128,8]{0,1:T(8,128)S(1)}, s32[128,8]{0,1:T(8,128)}, u32[]{:S(2)}) copy-start(s32[128,8]{0,1:T(8,128)} %param.25) | copy-start | bytes 12292
  24.6 18.9 %copy-start.4 = (s32[32]{0:T(128)S(1)}, s32[32]{0:T(128)}, u32[]{:S(2)}) copy-start(s32[32]{0:T(128)} %param.27) | copy-start | bytes 388
  24.6 41.6 %copy-start.5 = (bf16[128,2048]{1,0:T(8,128)(2,1)S(1)}, bf16[128,2048]{1,0:T(8,128)(2,1)}, u32[]{:S(2)}) copy-start(bf16[128,2048]{1,0:T(8,128)(2,1)} %param.16) | copy-start | bytes 1572868
  24.6 124.7 %all-to-all-start = ((bf16[32,128,256]{1,2,0:T(8,128)(2,1)}), bf16[32,128,256]{1,2,0:T(8,128)(2,1)S(1)}, u32[]{:S(2)}, u32[]{:S(2)}) async-start(bf16[32,128,256]{1,2,0:T(8,128)(2,1)} %copy.49), calls=%async_computation | async-start | bytes 4194304 | tf_op jit(solution)/shard_map/all_to_all | solution.py:17
  40.2 28.3 %copy-start.10 = (bf16[1024]{0:T(1024)(128)(2,1)S(1)}, bf16[1024]{0:T(1024)(128)(2,1)}, u32[]{:S(2)}) copy-start(bf16[1024]{0:T(1024)(128)(2,1)} %param.21) | copy-start | bytes 6148
  40.2 157.5 %all-gather.5.cloned.1.call-start = ((), (), s32[]{:S(2)}) async-start(), calls=%async_computation.4 | async-start | bytes 4325376 | tf_op jit(solution)/shard_map/all_gather | solution.py:135
  181.8 15.9 %copy-start.6 = (bf16[128,1024]{1,0:T(8,128)(2,1)S(1)}, bf16[128,1024]{1,0:T(8,128)(2,1)}, u32[]{:S(2)}) copy-start(bf16[128,1024]{1,0:T(8,128)(2,1)} %param.19) | copy-start | bytes 786436
  182.7 18.1 %copy-start.3 = (bf16[16,8,16,128]{3,1,2,0:T(8,128)(2,1)}, bf16[16,8,16,128]{3,1,2,0:T(8,128)(2,1)S(1)}, u32[]{:S(2)}) copy-start(bf16[16,8,16,128]{3,1,2,0:T(8,128)(2,1)S(1)} %copy.70) | copy-start | bytes 1572868
  197.7 3.0 copy-start.7
  216.5 155.6 %copy-start.11 = (bf16[1,1024,384]{2,1,0:T(8,128)(2,1)S(1)}, bf16[1,1024,384]{2,1,0:T(8,128)(2,1)}, u32[]{:S(2)}) copy-start(bf16[1,1024,384]{2,1,0:T(8,128)(2,1)} %param.22) | copy-start | bytes 2359300
  370.4 1.7 copy-start.2
  372.1 3.3 copy-start.12
  383.1 5.0 copy-start.9
  383.1 151.3 %all-to-all-start.2 = ((bf16[32,48,1024]{2,1,0:T(8,128)(2,1)}), bf16[32,48,1024]{2,1,0:T(8,128)(2,1)}, u32[]{:S(2)}, u32[]{:S(2)}) async-start(bf16[32,48,1024]{2,1,0:T(8,128)(2,1)} %bitcast.119), calls=%async_computation.2 | async-start | bytes 6291456 | tf_op jit(solution)/shard_map/all_to_all | solution.py:158
Sparse Core Ops, SparseCore 0:
  10.1 107.2 all-gather.2
  119.6 78.1 all-gather.4
